TPU v7x, 256 devices: a whole 4x4x8 slice. The times are simulated.
256 devices in a mesh: space: 16 (over z, y_lo), snap: 16 (over y_hi, x, core).
Axes of the slice: x: 4, y: 4 (y_hi: 2, y_lo: 2; y = y_hi * 2 + y_lo), z: 8, core: 2. Of those that a mesh axis runs over, the one named last changes fastest.
Arguments:
- primal: bfloat16 [2048, 196608], P('snap', 'space'), may hold values from -6 to 6
- adjoint_pencils: bfloat16 [1024, 196608], P('snap', 'space'), may hold values from -0.01953125 to 0.01953125
- weights: float32 [196608], P('space'), may hold values from 0.2 to 2
- pencil_map: int32 [1536], replicated, may hold values from 0 to 1535, as said below
Outputs:
- hankel: float32 [1024, 2048], P('space', 'snap')
Inputs may be any that keep to these rules, and one draw needn't show every extreme that they name: `pencil_map`: each number appears once; each aligned block of 96 entries holds exactly 6 entries from every aligned range of 96 values.
All inputs are finite; a program needn't handle non-finite values.
Results may differ from a plain program's by a relative error of at most 0.0029.
Values may be sent and summed in bfloat16 or wider, within the bound.
A program may use at most 128 MiB of HBM per device.

v0:
```python
import jax
import jax.numpy as jnp
from jax import lax
from jax.sharding import PartitionSpec as P

PEN_LEN = 128


def on_device(primal, adjoint_pencils, weights, pencil_map):
    rows_here = adjoint_pencils.shape[0]
    points = adjoint_pencils.shape[1]
    pen_dev = points // PEN_LEN
    tiles = lax.axis_size("space")
    share = pen_dev // tiles
    place = lax.axis_index("space")
    weighted = (primal.astype(jnp.float32) * weights[None, :]).astype(jnp.bfloat16)
    all_slots = pencil_map.reshape(tiles, pen_dev)
    targets = all_slots // pen_dev
    orders = jnp.argsort(targets, axis=1, stable=True)
    own_order = lax.dynamic_index_in_dim(orders, place, 0, keepdims=False)
    chosen = lax.dynamic_slice_in_dim(orders, place * share, share, 1)
    arrived = (jnp.take_along_axis(all_slots, chosen, axis=1) - place * pen_dev).reshape(pen_dev)
    blocks = adjoint_pencils.reshape(rows_here, pen_dev, PEN_LEN)
    outgoing = jnp.take(blocks, own_order, axis=1).reshape(rows_here, tiles, share, PEN_LEN)
    incoming = lax.all_to_all(outgoing, "space", split_axis=1, concat_axis=1, tiled=True)
    inverse = jnp.argsort(arrived)
    moving = jnp.take(incoming.reshape(rows_here, pen_dev, PEN_LEN), inverse, axis=1).reshape(
        rows_here, points
    )
    product = lax.dot_general(
        lax.all_gather(moving, "snap", axis=0, tiled=True),
        weighted,
        (((1,), (1,)), ((), ())),
        preferred_element_type=jnp.float32,
    )
    return lax.psum_scatter(product, "space", scatter_dimension=0, tiled=True)


def solution(mesh):
    placed = (P("snap", "space"), P("snap", "space"), P("space"), P())
    return jax.shard_map(
        on_device, mesh=mesh, in_specs=placed, out_specs=P("space", "snap"), check_vma=False
    )
```

profile of v0, /device:TPU:4, one launch (start us, length us, event | category | flops | bytes accessed | tf_op | source)
XLA Modules:
  0.0 308.7 jit_solution(8084344282338904994)
XLA Ops:
  6.5 0.0 copy-start
  6.5 0.9 reshape.38
  7.4 0.1 copy.12
  7.5 1.5 sort.34
  9.1 0.2 dynamic-slice_reduce_fusion
  9.3 0.0 copy-done
  9.3 0.4 copy_bitcast_fusion.1
  9.7 2.0 gather_fusion.1
  11.7 2.8 broadcast_select_fusion
  14.5 9.6 %all-to-all-start = ((bf16[64,16,6,128]{3,0,2,1:T(8,128)(2,1)}), bf16[64,16,6,128]{3,0,2,1:T(8,128)(2,1)S(1)}, u32[]{:S(2)}, u32[]{:S(2)}) async-start(bf16[64,16,6,128]{3,0,2,1:T(8,128)(2,1)} %bitcast.21), calls=%async_computation | async-start | bytes 3145728 | tf_op jit(solution)/shard_map/all_to_all | solution.py:25
  24.1 0.0 all-gather.2.cloned.1.call-start
  24.1 0.1 copy.13
  24.2 0.1 reshape.59
  24.3 1.2 gather_fusion
  25.6 0.1 reshape.62
  25.6 0.1 copy.14
  25.7 0.1 copy.15
  25.8 0.1 sub.19
  25.9 2.5 sort.35
  28.5 35.2 %all-to-all-done = bf16[64,16,6,128]{3,0,2,1:T(8,128)(2,1)S(1)} async-done(((bf16[64,16,6,128]{3,0,2,1:T(8,128)(2,1)}), bf16[64,16,6,128]{3,0,2,1:T(8,128)(2,1)S(1)}, u32[]{:S(2)}, u32[]{:S(2)}) %all-to-all-start) | async-done | bytes 1572896 | tf_op jit(solution)/shard_map/all_to_all | solution.py:25
  63.7 2.0 gather_fusion.2
  65.6 3.0 copy_bitcast_fusion
  68.6 0.0 copy-start.1
  68.6 0.0 all-gather.2.cloned.1.call-update
  68.6 0.0 reduce-scatter.2.cloned.1.call-start
  68.7 149.1 %all-gather.2.cloned.1.call-done = bf16[1024,12288]{1,0:T(8,128)(2,1)} async-done(((bf16[64,12288]{1,0:T(8,128)(2,1)}), bf16[1024,12288]{1,0:T(8,128)(2,1)}) %all-gather.2.cloned.1.call-update) | async-done | bytes 25165840 | tf_op jit(solution)/shard_map/all_gather | solution.py:31
  217.8 0.0 copy-done.1
  217.8 13.2 %fusion = f32[1024,128]{1,0:T(8,128)} fusion(bf16[1024,12288]{1,0:T(8,128)(2,1)} %all-gather.2.cloned.1.call-done, bf16[128,12288]{1,0:T(8,128)(2,1)} %param.6, f32[12288]{0:T(1024)S(1)} %copy-done.1), kind=kOutput, calls=%fused_computation.4 | convolution fusion | flops 3225944064 | bytes 28884992 | tf_op jit(solution)/shard_map/dot_general | solution.py:30
  231.0 0.0 reduce-scatter.2.cloned.1.call-update
  231.0 70.9 %reduce-scatter.2.cloned.1.call-done = f32[64,128]{1,0:T(8,128)} async-done(((f32[1024,128]{1,0:T(8,128)}), f32[64,128]{1,0:T(8,128)}) %reduce-scatter.2.cloned.1.call-update) | async-done | bytes 32784 | tf_op jit(solution)/shard_map/reduce_scatter | solution.py:36
  (11 shorter events, 0.1 us)
Async XLA Ops:
  6.5 2.7 copy-start
  14.5 49.2 %all-to-all-start = ((bf16[64,16,6,128]{3,0,2,1:T(8,128)(2,1)}), bf16[64,16,6,128]{3,0,2,1:T(8,128)(2,1)S(1)}, u32[]{:S(2)}, u32[]{:S(2)}) async-start(bf16[64,16,6,128]{3,0,2,1:T(8,128)(2,1)} %bitcast.21), calls=%async_computation | async-start | bytes 3145728 | tf_op jit(solution)/shard_map/all_to_all | solution.py:25
  24.1 193.7 %all-gather.2.cloned.1.call-start = ((), (), s32[]{:S(2)}) async-start(), calls=%async_computation.2 | async-start | bytes 26738688 | tf_op jit(solution)/shard_map/all_gather | solution.py:31
  68.6 149.2 %copy-start.1 = (f32[12288]{0:T(1024)S(1)}, f32[12288]{0:T(1024)}, u32[]{:S(2)}) copy-start(f32[12288]{0:T(1024)} %param.8) | copy-start | bytes 147460
  68.6 233.3 %reduce-scatter.2.cloned.1.call-start = ((), (), s32[]{:S(2)}) async-start(), calls=%async_computation.3 | async-start | bytes 557056 | tf_op jit(solution)/shard_map/reduce_scatter | solution.py:36
Sparse Core Ops, SparseCore 0:
  68.8 149.0 all-gather.1
  231.1 70.7 reduce-scatter.1
where the time goes:
time: 309 us
  waiting for transfers between devices  255 us (83%)
  between operations  13.5 us (4%)
  matrix products  13.2 us (4%)
  other arithmetic  9.89 us (3%)
  starting transfers between devices  9.67 us (3%)
  local copies, waits for them, and re-layouts  7.27 us (2%)
    all_gather x1, waiting for transfers between devices, on_device(): lax.all_gather(moving, 'snap', axis=0, tiled=True)  149 us
    reduce_scatter x1, waiting for transfers between devices, on_device(): return lax.psum_scatter(product, 'space', scatter_dimension=0, tiled=True)  70.9 us
    all_to_all x1, waiting for transfers between devices, on_device(): lax.all_to_all(outgoing, 'space', split_axis=1, concat_axis=1, tiled=True)  35.2 us
    dot_general x1, matrix products, on_device(): lax.dot_general(lax.all_gather(moving, 'snap', axis=0, tiled=True), weigh...  13.2 us
    all_to_all x1, starting transfers between devices, on_device(): lax.all_to_all(outgoing, 'space', split_axis=1, concat_axis=1, tiled=True)  9.58 us
  transfers between devices with their start and end apart: 3, of which 3 were waited for; matrix products, arithmetic and copies ran while one was open for 1% of the time, Pallas kernels for 0%

commit v1 on v0

--- a/solution.py
+++ b/solution.py
@@ -28,7 +28,9 @@
         rows_here, points
     )
     product = lax.dot_general(
-        lax.all_gather(moving, "snap", axis=0, tiled=True),
+        jnp.concatenate(
+            lax.all_to_all(jnp.stack([moving] * lax.axis_size("snap")), "snap", 0, 0), axis=0
+        ),
         weighted,
         (((1,), (1,)), ((), ())),
         preferred_element_type=jnp.float32,

time: 309 us -> 437 us (1.41)
  blocking collectives: 0 us -> 280 us
  waiting for transfers between devices: 255 us -> 103 us
    all_to_all x0 -> x1, blocking collectives: none -> 280 us  [on_device(): lax.all_to_all(jnp.stack([moving] * lax.axis_size('snap')), 'snap', 0, 0)]
    all_gather x1 -> x0, waiting for transfers between devices: 149 us -> none  [on_device(): lax.all_gather(moving, 'snap', axis=0, tiled=True)]
  transfers between devices with their start and end apart: 3 -> 2, of which waited for: 3 -> 2; matrix products, arithmetic and copies ran while one was open for 1% -> 1% of each run, Pallas kernels for 0% -> 0%
where the time goes in v1:
time: 437 us
  blocking collectives  280 us (64%)
  waiting for transfers between devices  103 us (24%)
  between operations  13.5 us (3%)
  matrix products  12.4 us (3%)
  local copies, waits for them, and re-layouts  10.2 us (2%)
  starting transfers between devices  9.62 us (2%)
  other arithmetic  8.65 us (2%)
    all_to_all x1, blocking collectives, on_device(): lax.all_to_all(jnp.stack([moving] * lax.axis_size('snap')), 'snap', 0, 0)  280 us
    reduce_scatter x1, waiting for transfers between devices, on_device(): return lax.psum_scatter(product, 'space', scatter_dimension=0, tiled=True)  67.6 us
    all_to_all x1, waiting for transfers between devices, on_device(): lax.all_to_all(outgoing, 'space', split_axis=1, concat_axis=1, tiled=True)  35.2 us
    dot_general x1, matrix products, on_device(): lax.dot_general(jnp.concatenate(lax.all_to_all(jnp.stack([moving] * lax.a...  12.4 us
    all_to_all x1, starting transfers between devices, on_device(): lax.all_to_all(outgoing, 'space', split_axis=1, concat_axis=1, tiled=True)  9.58 us
  transfers between devices with their start and end apart: 2, of which 2 were waited for; matrix products, arithmetic and copies ran while one was open for 1% of the time, Pallas kernels for 0%

profile of v1, /device:TPU:4, one launch (start us, length us, event | category | flops | bytes accessed | tf_op | source)
XLA Modules:
  0.0 437.2 jit_solution(9819858457399209294)
XLA Ops:
  6.5 0.0 copy-start
  6.5 0.9 reshape.40
  7.4 0.1 copy.12
  7.5 1.5 sort.34
  9.1 0.2 dynamic-slice_reduce_fusion
  9.3 0.0 copy-done
  9.3 0.4 copy_bitcast_fusion.1
  9.7 2.0 gather_fusion.1
  11.7 2.8 broadcast_select_fusion
  14.5 9.6 %all-to-all-start = ((bf16[64,16,6,128]{3,0,2,1:T(8,128)(2,1)}), bf16[64,16,6,128]{3,0,2,1:T(8,128)(2,1)S(1)}, u32[]{:S(2)}, u32[]{:S(2)}) async-start(bf16[64,16,6,128]{3,0,2,1:T(8,128)(2,1)} %bitcast.23), calls=%async_computation | async-start | bytes 3145728 | tf_op jit(solution)/shard_map/all_to_all | solution.py:25
  24.1 0.0 reduce-scatter.2.cloned.1.call-start
  24.1 0.1 copy.13
  24.2 0.1 reshape.61
  24.3 1.2 gather_fusion
  25.6 0.1 reshape.64
  25.6 0.1 copy.14
  25.7 0.1 copy.15
  25.8 0.1 sub.19
  25.9 2.5 sort.35
  28.5 35.2 %all-to-all-done = bf16[64,16,6,128]{3,0,2,1:T(8,128)(2,1)S(1)} async-done(((bf16[64,16,6,128]{3,0,2,1:T(8,128)(2,1)}), bf16[64,16,6,128]{3,0,2,1:T(8,128)(2,1)S(1)}, u32[]{:S(2)}, u32[]{:S(2)}) %all-to-all-start) | async-done | bytes 1572896 | tf_op jit(solution)/shard_map/all_to_all | solution.py:25
  63.7 2.0 gather_fusion.2
  65.6 1.7 copy_bitcast_fusion
  67.4 3.0 stack.3
  70.3 0.0 copy-start.1
  70.3 0.0 copy-start.2
  70.4 279.9 %all_to_all.10 = bf16[16,64,12288]{2,1,0:T(8,128)(2,1)} all-to-all(bf16[16,64,12288]{2,1,0:T(8,128)(2,1)S(1)} %stack.3), channel_id=1, replica_groups=mesh['space'=16,'snap'=16] {'snap'}, dimensions={0} | all-to-all | bytes 50331648 | tf_op jit(solution)/shard_map/all_to_all | solution.py:32
  350.3 0.0 copy-done.1
  350.3 0.0 copy-done.2
  350.3 12.4 %fusion = f32[1024,128]{1,0:T(8,128)} fusion(bf16[1024,12288]{1,0:T(8,128)(2,1)} %bitcast.21, bf16[128,12288]{1,0:T(8,128)(2,1)S(1)} %copy-done.1, f32[12288]{0:T(1024)S(1)} %copy-done.2), kind=kOutput, calls=%fused_computation.4 | convolution fusion | flops 3225944064 | bytes 28884992 | tf_op jit(solution)/shard_map/dot_general | solution.py:30
  362.7 0.0 reduce-scatter.2.cloned.1.call-update
  362.7 67.6 %reduce-scatter.2.cloned.1.call-done = f32[64,128]{1,0:T(8,128)} async-done(((f32[1024,128]{1,0:T(8,128)}), f32[64,128]{1,0:T(8,128)}) %reduce-scatter.2.cloned.1.call-update) | async-done | bytes 32784 | tf_op jit(solution)/shard_map/reduce_scatter | solution.py:38
  (11 shorter events, 0.1 us)
Async XLA Ops:
  6.5 2.7 copy-start
  14.5 49.2 %all-to-all-start = ((bf16[64,16,6,128]{3,0,2,1:T(8,128)(2,1)}), bf16[64,16,6,128]{3,0,2,1:T(8,128)(2,1)S(1)}, u32[]{:S(2)}, u32[]{:S(2)}) async-start(bf16[64,16,6,128]{3,0,2,1:T(8,128)(2,1)} %bitcast.23), calls=%async_computation | async-start | bytes 3145728 | tf_op jit(solution)/shard_map/all_to_all | solution.py:25
  24.1 406.3 %reduce-scatter.2.cloned.1.call-start = ((), (), s32[]{:S(2)}) async-start(), calls=%async_computation.3 | async-start | bytes 557056 | tf_op jit(solution)/shard_map/reduce_scatter | solution.py:38
  70.3 279.9 %copy-start.1 = (bf16[128,12288]{1,0:T(8,128)(2,1)S(1)}, bf16[128,12288]{1,0:T(8,128)(2,1)}, u32[]{:S(2)}) copy-start(bf16[128,12288]{1,0:T(8,128)(2,1)} %param.6) | copy-start | bytes 9437188
  70.3 279.9 %copy-start.2 = (f32[12288]{0:T(1024)S(1)}, f32[12288]{0:T(1024)}, u32[]{:S(2)}) copy-start(f32[12288]{0:T(1024)} %param.8) | copy-start | bytes 147460
Sparse Core Ops, SparseCore 0:
  362.8 67.4 reduce-scatter.1
